TPU v7x, 32 devices: a whole 2x2x4 slice. The times are simulated.
32 devices in a mesh: gz: 8 (over z, x), gy: 4 (over y, core).
Axes of the slice: x: 2, y: 2, z: 4, core: 2. Of those that a mesh axis runs over, the one named last changes fastest.
Arguments:
- parcel_cell: int32 [131072], P(('gz', 'gy')), may hold values from 0 to 131071
- parcel_offset: float32 [3, 131072], P(None, ('gz', 'gy')), may hold values from 0 to 1
- parcel_volume: float32 [131072], P(('gz', 'gy')), may hold values from 1 to 8
- parcel_force: float32 [3, 131072], P(None, ('gz', 'gy')), may hold values from -24 to 24
- brick_counts: int32 [8, 4], P('gz', 'gy'), may hold values from 1 to 4096, as said below
- divergence: float32 [64, 256, 256], P('gz', 'gy'), may hold values from -6 to 6
- pressure_prev: float32 [64, 256, 256], P('gz', 'gy'), may hold values from -6 to 6
- gas_density: float32 [64, 256, 256], P('gz', 'gy'), may hold values from 0.5 to 2
Outputs:
- gas_fraction: float32 [64, 256, 256], P('gz', 'gy')
- momentum_source: float32 [64, 3, 256, 256], P('gz', None, 'gy')
- pressure: float32 [64, 256, 256], P('gz', 'gy')
- residual: float32 [64, 256, 256], P('gz', 'gy')
Inputs may be any that keep to these rules, and one draw needn't show every extreme that they name: brick_counts gives the number of live parcels of each brick, held in the brick's first slots; one brick holds exactly 4096 and one exactly 1.
All inputs are finite; a program needn't handle non-finite values.
Results may differ from a plain program's by a relative error of at most 0.0021.
Values sent between devices are 32-bit elements; how exact they have to be, the bound alone decides.
A program may use at most 64 MiB of HBM per device.

v0:
```python
import jax
import jax.numpy as jnp
from jax import lax
from jax.sharding import PartitionSpec as P

CZ = 8
CY = 64
CX = 256
PCAP = 4096
SWEEPS = 3
ITERS = 2


smooth_rate = 0.15
stiffness = 0.002


def extended_2(cells, sides, width):
    for axis, dim in sides:
        count = lax.axis_size(axis)
        head = lax.slice_in_dim(cells, 0, width, axis=dim)
        tail = lax.slice_in_dim(cells, cells.shape[dim] - width, cells.shape[dim], axis=dim)
        cells = jnp.concatenate(
            [
                lax.ppermute(tail, axis, [(i, (i + 1) % count) for i in range(count)]),
                cells,
                lax.ppermute(head, axis, [((i + 1) % count, i) for i in range(count)]),
            ],
            axis=dim,
        )
    return cells


def tap_weight(distance):
    return jnp.exp(-0.5 * distance * distance)


def tap_norm(offset, home_cell, upper_bound):
    summed = jnp.zeros_like(offset)
    for shift_tap in range(-3, 4):
        inside = (home_cell + shift_tap >= 0) & (home_cell + shift_tap < upper_bound)
        summed = summed + jnp.where(inside, tap_weight(shift_tap + 0.5 - offset), 0.0)
    return summed


def plane_weights(planes, first_tap, home_cell, offset, norm_value, place_first, upper_bound):
    positions = jnp.arange(planes, dtype=jnp.int32)[:, None]
    tap_index = positions + first_tap - home_cell[None, :]
    places = positions + place_first
    active = (jnp.abs(tap_index) <= 3) & (places >= 0) & (places < upper_bound)
    distance = tap_index.astype(jnp.float32) + 0.5 - offset[None, :]
    return jnp.where(active, tap_weight(distance), 0.0) / norm_value[None, :]


def fold_edges(extended, axis_dim, lead_at, keep_len, reach_len):
    full_len = extended.shape[axis_dim]
    middle = lax.slice_in_dim(extended, lead_at, lead_at + keep_len, axis=axis_dim)
    head_part = lax.slice_in_dim(middle, 0, reach_len, axis=axis_dim) + lax.slice_in_dim(
        extended, 0, reach_len, axis=axis_dim
    )
    centre = lax.slice_in_dim(middle, reach_len, keep_len - reach_len, axis=axis_dim)
    tail_part = lax.slice_in_dim(
        middle, keep_len - reach_len, keep_len, axis=axis_dim
    ) + lax.slice_in_dim(extended, full_len - reach_len, full_len, axis=axis_dim)
    return jnp.concatenate([head_part, centre, tail_part], axis=axis_dim)


def wall_mask(values, row_first, row_total):
    places = row_first + jnp.arange(values.shape[2], dtype=jnp.int32)
    inside = ((places >= 0) & (places < row_total)).astype(jnp.float32)
    return values * inside[None, None, :, None]


def neighbours(values, row_first, row_total):
    extended = extended_2(values, (("gz", 0), ("gy", 2)), 1)
    return wall_mask(extended, row_first - 1, row_total)


def smooth_once(extended, row_first, row_total):
    centre = extended[1:-1, :, 1:-1]
    beside = (
        extended[2:, :, 1:-1]
        + extended[:-2, :, 1:-1]
        + extended[1:-1, :, 2:]
        + extended[1:-1, :, :-2]
    )
    padded = jnp.pad(centre, ((0, 0), (0, 0), (0, 0), (1, 1)))
    beside = beside + padded[..., 2:] + padded[..., :-2]
    places = row_first + jnp.arange(centre.shape[2], dtype=jnp.int32)
    columns = jnp.arange(centre.shape[3], dtype=jnp.int32)
    count_y = (places - 1 >= 0).astype(jnp.float32) + (places + 1 < row_total).astype(jnp.float32)
    count_x = (columns >= 1).astype(jnp.float32) + (columns <= centre.shape[3] - 2).astype(
        jnp.float32
    )
    neighbour_count = 2.0 + count_y[:, None] + count_x[None, :]
    return centre + smooth_rate * (beside - neighbour_count * centre)


def on_device(
    parcel_cell,
    parcel_offset,
    parcel_volume,
    parcel_force,
    brick_counts,
    divergence,
    pressure_prev,
    gas_density,
):
    row_first = lax.axis_index("gy") * CY
    row_total = lax.axis_size("gy") * CY
    slot_ids = jnp.arange(PCAP, dtype=jnp.int32)
    live_slots = (slot_ids < brick_counts[0, 0]).astype(jnp.float32)
    parcel_load = (
        jnp.concatenate([parcel_volume[None, :], parcel_volume[None, :] * parcel_force], axis=0)
        * live_slots[None, :]
    )
    cell_z = parcel_cell // (CY * CX)
    cell_y = parcel_cell // CX % CY
    cell_x = parcel_cell % CX
    norm_z = tap_norm(parcel_offset[0], cell_z * 0 + 3, 7)
    norm_y = tap_norm(parcel_offset[1], row_first + cell_y, row_total)
    norm_x = tap_norm(parcel_offset[2], cell_x, CX)
    weight_z = plane_weights(CZ + 6, -3, cell_z, parcel_offset[0], norm_z, 0, CZ + 6)
    weight_y = plane_weights(CY + 6, -3, cell_y, parcel_offset[1], norm_y, row_first - 3, row_total)
    weight_x = plane_weights(CX, 0, cell_x, parcel_offset[2], norm_x, 0, CX).astype(jnp.bfloat16)

    def deposit_plane(plane_weight):
        scaled = parcel_load * plane_weight[None, :]
        split_weight = (scaled[:, None, :] * weight_y[None, :, :]).astype(jnp.bfloat16)
        split_weight = split_weight.reshape(4 * (CY + 6), PCAP)
        summed = lax.dot_general(
            split_weight, weight_x, (((1,), (1,)), ((), ())), preferred_element_type=jnp.float32
        )
        return summed.reshape(4, CY + 6, CX)

    deposited = lax.map(deposit_plane, weight_z)
    extended = extended_2(deposited, (("gz", 0), ("gy", 2)), 3)
    summed_z = fold_edges(extended, 0, 6, CZ, 3)
    filtered = fold_edges(summed_z, 2, 6, CY, 3)
    for sweep_index in range(SWEEPS):
        filtered = smooth_once(neighbours(filtered, row_first, row_total), row_first, row_total)
    gas_fraction = 1.0 / (1.0 + filtered[:, 0])
    momentum = filtered[:, 1:]
    mobility = gas_fraction / gas_density
    stacked = jnp.concatenate([mobility[:, None], momentum], axis=1)
    beside_all = neighbours(stacked, row_first, row_total)
    mobility_x = jnp.pad(mobility, ((0, 0), (0, 0), (1, 1)))
    face_down = 0.5 * (mobility + beside_all[:-2, 0, 1:-1])
    face_up = 0.5 * (mobility + beside_all[2:, 0, 1:-1])
    face_south = 0.5 * (mobility + beside_all[1:-1, 0, :-2])
    face_north = 0.5 * (mobility + beside_all[1:-1, 0, 2:])
    face_west = 0.5 * (mobility + mobility_x[..., :-2])
    face_east = 0.5 * (mobility + mobility_x[..., 2:])
    diagonal = (
        stiffness * mobility + face_down + face_up + face_south + face_north + face_west + face_east
    )
    force_x = jnp.pad(momentum[:, 2], ((0, 0), (0, 0), (1, 1)))
    spread = (
        0.5 * (beside_all[2:, 1, 1:-1] - beside_all[:-2, 1, 1:-1])
        + 0.5 * (beside_all[1:-1, 2, 2:] - beside_all[1:-1, 2, :-2])
        + 0.5 * (force_x[..., 2:] - force_x[..., :-2])
    )
    right_side = divergence - spread

    def operate(values):
        around_p = neighbours(values[:, None], row_first, row_total)
        padded_x = jnp.pad(values, ((0, 0), (0, 0), (1, 1)))
        coupled = (
            face_down * around_p[:-2, 0, 1:-1]
            + face_up * around_p[2:, 0, 1:-1]
            + face_south * around_p[1:-1, 0, :-2]
            + face_north * around_p[1:-1, 0, 2:]
            + face_west * padded_x[..., :-2]
            + face_east * padded_x[..., 2:]
        )
        return diagonal * values - coupled

    def paired(residual_now, scaled_vec, mapped_vec):
        return lax.psum(
            (jnp.sum(residual_now * scaled_vec), jnp.sum(scaled_vec * mapped_vec)), ("gz", "gy")
        )

    solution = pressure_prev
    residual = right_side - operate(solution)
    precond = residual / diagonal
    mapped = operate(precond)
    scaled_norm, curvature = paired(residual, precond, mapped)
    step_size = scaled_norm / curvature
    direction, mapped_dir = (precond, mapped)
    for iteration in range(ITERS):
        solution = solution + step_size * direction
        residual = residual - step_size * mapped_dir
        if iteration + 1 < ITERS:
            precond = residual / diagonal
            mapped = operate(precond)
            norm_next, curvature = paired(residual, precond, mapped)
            beta_ratio = norm_next / scaled_norm
            step_size = norm_next / (curvature - beta_ratio * norm_next / step_size)
            direction = precond + beta_ratio * direction
            mapped_dir = mapped + beta_ratio * mapped_dir
            scaled_norm = norm_next
    return (gas_fraction, momentum, solution, residual)


def solution(mesh):
    return jax.shard_map(
        on_device,
        mesh=mesh,
        in_specs=(
            P(("gz", "gy")),
            P(None, ("gz", "gy")),
            P(("gz", "gy")),
            P(None, ("gz", "gy")),
            P("gz", "gy"),
            P("gz", "gy", None),
            P("gz", "gy", None),
            P("gz", "gy", None),
        ),
        out_specs=(
            P("gz", "gy", None),
            P("gz", None, "gy", None),
            P("gz", "gy", None),
            P("gz", "gy", None),
        ),
        check_vma=False,
    )
```

profile of v0, /device:TPU:0, one launch (start us, length us, event | category | flops | bytes accessed | tf_op | source)
XLA Modules:
  0.0 334.4 jit_solution(5600878162469630291)
XLA Ops:
  5.9 64.2 %while.11 = (s32[]{:T(128)}, f32[14,4,70,256]{3,2,1,0:T(8,128)}, f32[14,4096]{1,0:T(8,128)S(1)}, f32[4,4096]{1,0:T(4,128)S(1)}, pred[70]{0:T(512)(128)(4,1)S(1)}...) while((s32[]{:T(128)}, f32[14,4,70,256]{3,2,1,0:T(8,128)}, ...), condition=%wide.region_1.2_spmd.clone, body=%wide.region_0.1_spmd.clone.sunk | while | flops 605536256 | bytes 2934069 | solution.py:136
  11.4 3.8 %fusion.201 = f32[14,4,70,256]{3,2,1,0:T(8,128)} fusion(f32[14,4,70,256]{3,2,1,0:T(8,128)} %get-tuple-element.276, s32[]{:T(128)} %get-tuple-element.275, f32[4096]{0:T(1024)S(1)} %get-tuple-element.303, f32[4096]{0:T(1024)S(1)} %get-tuple-element.302, s32[4096]{0:T(1024)S(1)} %get-tuple-element.301, pred[256]{0:T(512)(128)(4,1)S(1)} %get-tuple-element.300, ...), kind=kOutput, calls=%fused_computation.35.clone.1 | convolution fusion | flops 602079232 | bytes 1557248 | tf_op jit(solution)/shard_map/while/body/eval_jaxpr/dot_general | solution.py:131
  15.9 3.8 %fusion.201 = f32[14,4,70,256]{3,2,1,0:T(8,128)} fusion(f32[14,4,70,256]{3,2,1,0:T(8,128)} %get-tuple-element.276, s32[]{:T(128)} %get-tuple-element.275, f32[4096]{0:T(1024)S(1)} %get-tuple-element.303, f32[4096]{0:T(1024)S(1)} %get-tuple-element.302, s32[4096]{0:T(1024)S(1)} %get-tuple-element.301, pred[256]{0:T(512)(128)(4,1)S(1)} %get-tuple-element.300, ...), kind=kOutput, calls=%fused_computation.35.clone.1 | convolution fusion | flops 602079232 | bytes 1557248 | tf_op jit(solution)/shard_map/while/body/eval_jaxpr/dot_general | solution.py:131
  20.5 3.8 %fusion.201 = f32[14,4,70,256]{3,2,1,0:T(8,128)} fusion(f32[14,4,70,256]{3,2,1,0:T(8,128)} %get-tuple-element.276, s32[]{:T(128)} %get-tuple-element.275, f32[4096]{0:T(1024)S(1)} %get-tuple-element.303, f32[4096]{0:T(1024)S(1)} %get-tuple-element.302, s32[4096]{0:T(1024)S(1)} %get-tuple-element.301, pred[256]{0:T(512)(128)(4,1)S(1)} %get-tuple-element.300, ...), kind=kOutput, calls=%fused_computation.35.clone.1 | convolution fusion | flops 602079232 | bytes 1557248 | tf_op jit(solution)/shard_map/while/body/eval_jaxpr/dot_general | solution.py:131
  25.1 3.8 %fusion.201 = f32[14,4,70,256]{3,2,1,0:T(8,128)} fusion(f32[14,4,70,256]{3,2,1,0:T(8,128)} %get-tuple-element.276, s32[]{:T(128)} %get-tuple-element.275, f32[4096]{0:T(1024)S(1)} %get-tuple-element.303, f32[4096]{0:T(1024)S(1)} %get-tuple-element.302, s32[4096]{0:T(1024)S(1)} %get-tuple-element.301, pred[256]{0:T(512)(128)(4,1)S(1)} %get-tuple-element.300, ...), kind=kOutput, calls=%fused_computation.35.clone.1 | convolution fusion | flops 602079232 | bytes 1557248 | tf_op jit(solution)/shard_map/while/body/eval_jaxpr/dot_general | solution.py:131
  38.9 3.8 %fusion.201 = f32[14,4,70,256]{3,2,1,0:T(8,128)} fusion(f32[14,4,70,256]{3,2,1,0:T(8,128)} %get-tuple-element.276, s32[]{:T(128)} %get-tuple-element.275, f32[4096]{0:T(1024)S(1)} %get-tuple-element.303, f32[4096]{0:T(1024)S(1)} %get-tuple-element.302, s32[4096]{0:T(1024)S(1)} %get-tuple-element.301, pred[256]{0:T(512)(128)(4,1)S(1)} %get-tuple-element.300, ...), kind=kOutput, calls=%fused_computation.35.clone.1 | convolution fusion | flops 602079232 | bytes 1557248 | tf_op jit(solution)/shard_map/while/body/eval_jaxpr/dot_general | solution.py:131
  43.5 3.8 %fusion.201 = f32[14,4,70,256]{3,2,1,0:T(8,128)} fusion(f32[14,4,70,256]{3,2,1,0:T(8,128)} %get-tuple-element.276, s32[]{:T(128)} %get-tuple-element.275, f32[4096]{0:T(1024)S(1)} %get-tuple-element.303, f32[4096]{0:T(1024)S(1)} %get-tuple-element.302, s32[4096]{0:T(1024)S(1)} %get-tuple-element.301, pred[256]{0:T(512)(128)(4,1)S(1)} %get-tuple-element.300, ...), kind=kOutput, calls=%fused_computation.35.clone.1 | convolution fusion | flops 602079232 | bytes 1557248 | tf_op jit(solution)/shard_map/while/body/eval_jaxpr/dot_general | solution.py:131
  48.0 3.8 %fusion.201 = f32[14,4,70,256]{3,2,1,0:T(8,128)} fusion(f32[14,4,70,256]{3,2,1,0:T(8,128)} %get-tuple-element.276, s32[]{:T(128)} %get-tuple-element.275, f32[4096]{0:T(1024)S(1)} %get-tuple-element.303, f32[4096]{0:T(1024)S(1)} %get-tuple-element.302, s32[4096]{0:T(1024)S(1)} %get-tuple-element.301, pred[256]{0:T(512)(128)(4,1)S(1)} %get-tuple-element.300, ...), kind=kOutput, calls=%fused_computation.35.clone.1 | convolution fusion | flops 602079232 | bytes 1557248 | tf_op jit(solution)/shard_map/while/body/eval_jaxpr/dot_general | solution.py:131
  52.6 3.8 %fusion.201 = f32[14,4,70,256]{3,2,1,0:T(8,128)} fusion(f32[14,4,70,256]{3,2,1,0:T(8,128)} %get-tuple-element.276, s32[]{:T(128)} %get-tuple-element.275, f32[4096]{0:T(1024)S(1)} %get-tuple-element.303, f32[4096]{0:T(1024)S(1)} %get-tuple-element.302, s32[4096]{0:T(1024)S(1)} %get-tuple-element.301, pred[256]{0:T(512)(128)(4,1)S(1)} %get-tuple-element.300, ...), kind=kOutput, calls=%fused_computation.35.clone.1 | convolution fusion | flops 602079232 | bytes 1557248 | tf_op jit(solution)/shard_map/while/body/eval_jaxpr/dot_general | solution.py:131
  61.8 3.8 %fusion.201 = f32[14,4,70,256]{3,2,1,0:T(8,128)} fusion(f32[14,4,70,256]{3,2,1,0:T(8,128)} %get-tuple-element.276, s32[]{:T(128)} %get-tuple-element.275, f32[4096]{0:T(1024)S(1)} %get-tuple-element.303, f32[4096]{0:T(1024)S(1)} %get-tuple-element.302, s32[4096]{0:T(1024)S(1)} %get-tuple-element.301, pred[256]{0:T(512)(128)(4,1)S(1)} %get-tuple-element.300, ...), kind=kOutput, calls=%fused_computation.35.clone.1 | convolution fusion | flops 602079232 | bytes 1557248 | tf_op jit(solution)/shard_map/while/body/eval_jaxpr/dot_general | solution.py:131
  80.3 33.7 %collective-permute-done = f32[3,4,70,256]{3,1,2,0:T(4,128)S(1)} collective-permute-done((f32[3,4,70,256]{3,1,2,0:T(4,128)S(1)}, f32[3,4,70,256]{3,1,2,0:T(4,128)S(1)}, u32[]{:S(2)}, u32[]{:S(2)}) %collective-permute-start) | collective-permute-done | bytes 860192 | tf_op jit(solution)/shard_map/ppermute | solution.py:25
  118.2 6.4 %collective-permute-done.2 = f32[20,4,3,256]{3,2,0,1:T(4,128)S(1)} collective-permute-done((f32[20,4,3,256]{3,2,0,1:T(4,128)S(1)}, f32[20,4,3,256]{3,2,0,1:T(4,128)S(1)}, u32[]{:S(2)}, u32[]{:S(2)}) %collective-permute-start.2) | collective-permute-done | bytes 245792 | tf_op jit(solution)/shard_map/ppermute | solution.py:25
  128.2 3.8 %collective-permute-start.5 = (f32[1,4,64,256]{3,2,0,1:T(8,128)S(1)}, f32[1,4,64,256]{3,2,0,1:T(8,128)S(1)}, u32[]{:S(2)}, u32[]{:S(2)}) collective-permute-start(f32[1,4,64,256]{3,2,0,1:T(8,128)S(1)} %get-tuple-element.145), channel_id=1, source_target_pairs={{4,0},{8,4},{12,8},{16,12},{20,16},{24,20},{28,24},{0,28},{5,1},{9... | collective-permute-start | bytes 786440 | tf_op jit(solution)/shard_map/ppermute | solution.py:27
  132.2 8.5 %collective-permute-done.4 = f32[1,4,64,256]{3,2,0,1:T(8,128)S(1)} collective-permute-done((f32[1,4,64,256]{3,2,0,1:T(8,128)}, f32[1,4,64,256]{3,2,0,1:T(8,128)S(1)}, u32[]{:S(2)}, u32[]{:S(2)}) %collective-permute-start.4) | collective-permute-done | bytes 262176 | tf_op jit(solution)/shard_map/ppermute | solution.py:25
  148.8 4.3 %collective-permute-start.9 = (f32[1,4,64,256]{3,2,0,1:T(8,128)S(1)}, f32[1,4,64,256]{3,2,0,1:T(8,128)S(1)}, u32[]{:S(2)}, u32[]{:S(2)}) collective-permute-start(f32[1,4,64,256]{3,2,0,1:T(8,128)S(1)} %get-tuple-element.153), channel_id=1, source_target_pairs={{4,0},{8,4},{12,8},{16,12},{20,16},{24,20},{28,24},{0,28},{5,1},{9... | collective-permute-start | bytes 786440 | tf_op jit(solution)/shard_map/ppermute | solution.py:27
  153.1 7.3 %collective-permute-done.8 = f32[1,4,64,256]{3,2,0,1:T(8,128)S(1)} collective-permute-done((f32[1,4,64,256]{3,2,0,1:T(8,128)S(1)}, f32[1,4,64,256]{3,2,0,1:T(8,128)S(1)}, u32[]{:S(2)}, u32[]{:S(2)}) %collective-permute-start.8) | collective-permute-done | bytes 262176 | tf_op jit(solution)/shard_map/ppermute | solution.py:25
  169.2 4.7 %collective-permute-start.13 = (f32[1,4,64,256]{3,2,0,1:T(8,128)S(1)}, f32[1,4,64,256]{3,2,0,1:T(8,128)S(1)}, u32[]{:S(2)}, u32[]{:S(2)}) collective-permute-start(f32[1,4,64,256]{3,2,0,1:T(8,128)S(1)} %get-tuple-element.151), channel_id=1, source_target_pairs={{4,0},{8,4},{12,8},{16,12},{20,16},{24,20},{28,24},{0,28},{5,1},{9... | collective-permute-start | bytes 786440 | tf_op jit(solution)/shard_map/ppermute | solution.py:27
  173.9 6.3 %collective-permute-done.12 = f32[1,4,64,256]{3,2,0,1:T(8,128)S(1)} collective-permute-done((f32[1,4,64,256]{3,2,0,1:T(8,128)S(1)}, f32[1,4,64,256]{3,2,0,1:T(8,128)S(1)}, u32[]{:S(2)}, u32[]{:S(2)}) %collective-permute-start.12) | collective-permute-done | bytes 262176 | tf_op jit(solution)/shard_map/ppermute | solution.py:25
  180.1 4.9 %collective-permute-done.13 = f32[1,4,64,256]{3,2,0,1:T(8,128)S(1)} collective-permute-done((f32[1,4,64,256]{3,2,0,1:T(8,128)S(1)}, f32[1,4,64,256]{3,2,0,1:T(8,128)S(1)}, u32[]{:S(2)}, u32[]{:S(2)}) %collective-permute-start.13) | collective-permute-done | bytes 262176 | tf_op jit(solution)/shard_map/ppermute | solution.py:27
  187.0 4.7 %collective-permute-start.21 = (f32[1,1,64,256]{3,2,0,1:T(8,128)S(1)}, f32[1,1,64,256]{3,2,0,1:T(8,128)S(1)}, u32[]{:S(2)}, u32[]{:S(2)}) collective-permute-start(f32[1,1,64,256]{3,2,0,1:T(8,128)S(1)} %get-tuple-element.165), channel_id=1, source_target_pairs={{4,0},{8,4},{12,8},{16,12},{20,16},{24,20},{28,24},{0,28},{5,1},{9... | collective-permute-start | bytes 196616 | tf_op jit(solution)/shard_map/ppermute | solution.py:27
  195.9 4.7 %collective-permute-start.17 = (f32[1,4,64,256]{3,2,0,1:T(8,128)S(1)}, f32[1,4,64,256]{3,2,0,1:T(8,128)S(1)}, u32[]{:S(2)}, u32[]{:S(2)}) collective-permute-start(f32[1,4,64,256]{3,2,0,1:T(8,128)S(1)} %get-tuple-element.147), channel_id=1, source_target_pairs={{4,0},{8,4},{12,8},{16,12},{20,16},{24,20},{28,24},{0,28},{5,1},{9... | collective-permute-start | bytes 786440 | tf_op jit(solution)/shard_map/ppermute | solution.py:27
  214.8 4.5 %collective-permute-start.25 = (f32[1,1,64,256]{3,2,0,1:T(8,128)S(1)}, f32[1,1,64,256]{3,2,0,1:T(8,128)S(1)}, u32[]{:S(2)}, u32[]{:S(2)}) collective-permute-start(f32[1,1,64,256]{3,2,0,1:T(8,128)S(1)} %get-tuple-element.163), channel_id=1, source_target_pairs={{4,0},{8,4},{12,8},{16,12},{20,16},{24,20},{28,24},{0,28},{5,1},{9... | collective-permute-start | bytes 196616 | tf_op jit(solution)/shard_map/ppermute | solution.py:27
  227.9 39.7 %all-reduce.9 = (f32[]{:T(128)}, f32[]{:T(128)}) all-reduce(f32[]{:T(128)} %get-tuple-element.89, f32[]{:T(128)} %get-tuple-element.88), channel_id=1, replica_groups=mesh['gz'=8,'gy'=4] {'gz','gy'}, use_global_device_ids=true, to_apply=%region_3.4 | all-reduce | flops 2 | bytes 16 | tf_op jit(solution)/shard_map/psum | solution.py:179
  283.8 41.4 %all-reduce.8 = (f32[]{:T(128)}, f32[]{:T(128)}) all-reduce(f32[]{:T(128)} %get-tuple-element.87, f32[]{:T(128)} %get-tuple-element.86), channel_id=1, replica_groups=mesh['gz'=8,'gy'=4] {'gz','gy'}, use_global_device_ids=true, to_apply=%region_7.8 | all-reduce | flops 2 | bytes 16 | tf_op jit(solution)/shard_map/psum | solution.py:179
  (185 shorter events, 117.4 us)
Async XLA Ops:
  74.1 39.8 %collective-permute-start = (f32[3,4,70,256]{3,1,2,0:T(4,128)S(1)}, f32[3,4,70,256]{3,1,2,0:T(4,128)S(1)}, u32[]{:S(2)}, u32[]{:S(2)}) collective-permute-start(f32[3,4,70,256]{3,1,2,0:T(4,128)S(1)} %get-tuple-element.133), channel_id=1, source_target_pairs={{0,4},{4,8},{8,12},{12,16},{16,20},{20,24},{24,28},{28,0},{1,5},{5... | collective-permute-start | bytes 2580488 | tf_op jit(solution)/shard_map/ppermute | solution.py:25
  77.2 39.0 %collective-permute-start.1 = (f32[3,4,70,256]{3,1,2,0:T(4,128)S(1)}, f32[3,4,70,256]{3,1,2,0:T(4,128)S(1)}, u32[]{:S(2)}, u32[]{:S(2)}) collective-permute-start(f32[3,4,70,256]{3,1,2,0:T(4,128)S(1)} %get-tuple-element.132), channel_id=1, source_target_pairs={{4,0},{8,4},{12,8},{16,12},{20,16},{24,20},{28,24},{0,28},{5,1},{9... | collective-permute-start | bytes 2580488 | tf_op jit(solution)/shard_map/ppermute | solution.py:27
  116.4 8.2 %collective-permute-start.2 = (f32[20,4,3,256]{3,2,0,1:T(4,128)S(1)}, f32[20,4,3,256]{3,2,0,1:T(4,128)S(1)}, u32[]{:S(2)}, u32[]{:S(2)}) collective-permute-start(f32[20,4,3,256]{3,2,0,1:T(4,128)S(1)} %get-tuple-element.130), channel_id=1, source_target_pairs={{0,1},{1,2},{2,3},{3,0},{4,5},{5,6},{6,7},{7,4},{8,9},{9,10},{10,1... | collective-permute-start | bytes 737288 | tf_op jit(solution)/shard_map/ppermute | solution.py:25
  116.5 9.0 %collective-permute-start.3 = (f32[20,4,3,256]{3,2,0,1:T(4,128)S(1)}, f32[20,4,3,256]{3,2,0,1:T(4,128)S(1)}, u32[]{:S(2)}, u32[]{:S(2)}) collective-permute-start(f32[20,4,3,256]{3,2,0,1:T(4,128)S(1)} %get-tuple-element.131), channel_id=1, source_target_pairs={{1,0},{2,1},{3,2},{0,3},{5,4},{6,5},{7,6},{4,7},{9,8},{10,9},{11,1... | collective-permute-start | bytes 737288 | tf_op jit(solution)/shard_map/ppermute | solution.py:27
  127.4 13.3 %collective-permute-start.4 = (f32[1,4,64,256]{3,2,0,1:T(8,128)}, f32[1,4,64,256]{3,2,0,1:T(8,128)S(1)}, u32[]{:S(2)}, u32[]{:S(2)}) collective-permute-start(f32[1,4,64,256]{3,2,0,1:T(8,128)} %get-tuple-element.144), channel_id=1, source_target_pairs={{0,4},{4,8},{8,12},{12,16},{16,20},{20,24},{24,28},{28,0},{1,5},{5... | collective-permute-start | bytes 786440 | tf_op jit(solution)/shard_map/ppermute | solution.py:25
  128.2 14.4 %collective-permute-start.5 = (f32[1,4,64,256]{3,2,0,1:T(8,128)S(1)}, f32[1,4,64,256]{3,2,0,1:T(8,128)S(1)}, u32[]{:S(2)}, u32[]{:S(2)}) collective-permute-start(f32[1,4,64,256]{3,2,0,1:T(8,128)S(1)} %get-tuple-element.145), channel_id=1, source_target_pairs={{4,0},{8,4},{12,8},{16,12},{20,16},{24,20},{28,24},{0,28},{5,1},{9... | collective-permute-start | bytes 786440 | tf_op jit(solution)/shard_map/ppermute | solution.py:27
  142.8 3.5 %collective-permute-start.6 = (f32[10,4,1,256]{3,2,0,1:T(1,128)S(1)}, f32[10,4,1,256]{3,2,0,1:T(1,128)S(1)}, u32[]{:S(2)}, u32[]{:S(2)}) collective-permute-start(f32[10,4,1,256]{3,2,0,1:T(1,128)S(1)} %get-tuple-element.134), channel_id=1, source_target_pairs={{0,1},{1,2},{2,3},{3,0},{4,5},{5,6},{6,7},{7,4},{8,9},{9,10},{10,1... | collective-permute-start | bytes 122888 | tf_op jit(solution)/shard_map/ppermute | solution.py:25
  142.9 3.4 %collective-permute-start.7 = (f32[10,4,1,256]{3,2,0,1:T(1,128)S(1)}, f32[10,4,1,256]{3,2,0,1:T(1,128)S(1)}, u32[]{:S(2)}, u32[]{:S(2)}) collective-permute-start(f32[10,4,1,256]{3,2,0,1:T(1,128)S(1)} %get-tuple-element.135), channel_id=1, source_target_pairs={{1,0},{2,1},{3,2},{0,3},{5,4},{6,5},{7,6},{4,7},{9,8},{10,9},{11,1... | collective-permute-start | bytes 122888 | tf_op jit(solution)/shard_map/ppermute | solution.py:27
  148.3 12.1 %collective-permute-start.8 = (f32[1,4,64,256]{3,2,0,1:T(8,128)S(1)}, f32[1,4,64,256]{3,2,0,1:T(8,128)S(1)}, u32[]{:S(2)}, u32[]{:S(2)}) collective-permute-start(f32[1,4,64,256]{3,2,0,1:T(8,128)S(1)} %get-tuple-element.152), channel_id=1, source_target_pairs={{0,4},{4,8},{8,12},{12,16},{16,20},{20,24},{24,28},{28,0},{1,5},{5... | collective-permute-start | bytes 786440 | tf_op jit(solution)/shard_map/ppermute | solution.py:25
  148.8 14.8 %collective-permute-start.9 = (f32[1,4,64,256]{3,2,0,1:T(8,128)S(1)}, f32[1,4,64,256]{3,2,0,1:T(8,128)S(1)}, u32[]{:S(2)}, u32[]{:S(2)}) collective-permute-start(f32[1,4,64,256]{3,2,0,1:T(8,128)S(1)} %get-tuple-element.153), channel_id=1, source_target_pairs={{4,0},{8,4},{12,8},{16,12},{20,16},{24,20},{28,24},{0,28},{5,1},{9... | collective-permute-start | bytes 786440 | tf_op jit(solution)/shard_map/ppermute | solution.py:27
  163.6 3.5 %collective-permute-start.10 = (f32[10,4,1,256]{3,2,0,1:T(1,128)S(1)}, f32[10,4,1,256]{3,2,0,1:T(1,128)S(1)}, u32[]{:S(2)}, u32[]{:S(2)}) collective-permute-start(f32[10,4,1,256]{3,2,0,1:T(1,128)S(1)} %get-tuple-element.140), channel_id=1, source_target_pairs={{0,1},{1,2},{2,3},{3,0},{4,5},{5,6},{6,7},{7,4},{8,9},{9,10},{10,1... | collective-permute-start | bytes 122888 | tf_op jit(solution)/shard_map/ppermute | solution.py:25
  169.1 11.1 %collective-permute-start.12 = (f32[1,4,64,256]{3,2,0,1:T(8,128)S(1)}, f32[1,4,64,256]{3,2,0,1:T(8,128)S(1)}, u32[]{:S(2)}, u32[]{:S(2)}) collective-permute-start(f32[1,4,64,256]{3,2,0,1:T(8,128)S(1)} %get-tuple-element.150), channel_id=1, source_target_pairs={{0,4},{4,8},{8,12},{12,16},{16,20},{20,24},{24,28},{28,0},{1,5},{5... | collective-permute-start | bytes 786440 | tf_op jit(solution)/shard_map/ppermute | solution.py:25
  169.2 15.9 %collective-permute-start.13 = (f32[1,4,64,256]{3,2,0,1:T(8,128)S(1)}, f32[1,4,64,256]{3,2,0,1:T(8,128)S(1)}, u32[]{:S(2)}, u32[]{:S(2)}) collective-permute-start(f32[1,4,64,256]{3,2,0,1:T(8,128)S(1)} %get-tuple-element.151), channel_id=1, source_target_pairs={{4,0},{8,4},{12,8},{16,12},{20,16},{24,20},{28,24},{0,28},{5,1},{9... | collective-permute-start | bytes 786440 | tf_op jit(solution)/shard_map/ppermute | solution.py:27
  185.1 6.6 %collective-permute-start.14 = (f32[10,4,1,256]{3,2,0,1:T(1,128)S(1)}, f32[10,4,1,256]{3,2,0,1:T(1,128)S(1)}, u32[]{:S(2)}, u32[]{:S(2)}) collective-permute-start(f32[10,4,1,256]{3,2,0,1:T(1,128)S(1)} %get-tuple-element.138), channel_id=1, source_target_pairs={{0,1},{1,2},{2,3},{3,0},{4,5},{5,6},{6,7},{7,4},{8,9},{9,10},{10,1... | collective-permute-start | bytes 122888 | tf_op jit(solution)/shard_map/ppermute | solution.py:25
  185.4 6.3 %collective-permute-start.15 = (f32[10,4,1,256]{3,2,0,1:T(1,128)S(1)}, f32[10,4,1,256]{3,2,0,1:T(1,128)S(1)}, u32[]{:S(2)}, u32[]{:S(2)}) collective-permute-start(f32[10,4,1,256]{3,2,0,1:T(1,128)S(1)} %get-tuple-element.139), channel_id=1, source_target_pairs={{1,0},{2,1},{3,2},{0,3},{5,4},{6,5},{7,6},{4,7},{9,8},{10,9},{11,1... | collective-permute-start | bytes 122888 | tf_op jit(solution)/shard_map/ppermute | solution.py:27
  186.9 13.7 %collective-permute-start.20 = (f32[1,1,64,256]{3,2,0,1:T(8,128)S(1)}, f32[1,1,64,256]{3,2,0,1:T(8,128)S(1)}, u32[]{:S(2)}, u32[]{:S(2)}) collective-permute-start(f32[1,1,64,256]{3,2,0,1:T(8,128)S(1)} %get-tuple-element.164), channel_id=1, source_target_pairs={{0,4},{4,8},{8,12},{12,16},{16,20},{20,24},{24,28},{28,0},{1,5},{5... | collective-permute-start | bytes 196616 | tf_op jit(solution)/shard_map/ppermute | solution.py:25
  187.0 13.6 %collective-permute-start.21 = (f32[1,1,64,256]{3,2,0,1:T(8,128)S(1)}, f32[1,1,64,256]{3,2,0,1:T(8,128)S(1)}, u32[]{:S(2)}, u32[]{:S(2)}) collective-permute-start(f32[1,1,64,256]{3,2,0,1:T(8,128)S(1)} %get-tuple-element.165), channel_id=1, source_target_pairs={{4,0},{8,4},{12,8},{16,12},{20,16},{24,20},{28,24},{0,28},{5,1},{9... | collective-permute-start | bytes 196616 | tf_op jit(solution)/shard_map/ppermute | solution.py:27
  195.8 11.0 %collective-permute-start.16 = (f32[1,4,64,256]{3,2,0,1:T(8,128)S(1)}, f32[1,4,64,256]{3,2,0,1:T(8,128)S(1)}, u32[]{:S(2)}, u32[]{:S(2)}) collective-permute-start(f32[1,4,64,256]{3,2,0,1:T(8,128)S(1)} %get-tuple-element.146), channel_id=1, source_target_pairs={{0,4},{4,8},{8,12},{12,16},{16,20},{20,24},{24,28},{28,0},{1,5},{5... | collective-permute-start | bytes 786440 | tf_op jit(solution)/shard_map/ppermute | solution.py:25
  195.9 13.3 %collective-permute-start.17 = (f32[1,4,64,256]{3,2,0,1:T(8,128)S(1)}, f32[1,4,64,256]{3,2,0,1:T(8,128)S(1)}, u32[]{:S(2)}, u32[]{:S(2)}) collective-permute-start(f32[1,4,64,256]{3,2,0,1:T(8,128)S(1)} %get-tuple-element.147), channel_id=1, source_target_pairs={{4,0},{8,4},{12,8},{16,12},{20,16},{24,20},{28,24},{0,28},{5,1},{9... | collective-permute-start | bytes 786440 | tf_op jit(solution)/shard_map/ppermute | solution.py:27
  209.2 3.5 %collective-permute-start.18 = (f32[10,4,1,256]{3,2,0,1:T(1,128)S(1)}, f32[10,4,1,256]{3,2,0,1:T(1,128)S(1)}, u32[]{:S(2)}, u32[]{:S(2)}) collective-permute-start(f32[10,4,1,256]{3,2,0,1:T(1,128)S(1)} %get-tuple-element.136), channel_id=1, source_target_pairs={{0,1},{1,2},{2,3},{3,0},{4,5},{5,6},{6,7},{7,4},{8,9},{9,10},{10,1... | collective-permute-start | bytes 122888 | tf_op jit(solution)/shard_map/ppermute | solution.py:25
  214.5 7.7 %collective-permute-start.24 = (f32[1,1,64,256]{3,2,0,1:T(8,128)S(1)}, f32[1,1,64,256]{3,2,0,1:T(8,128)S(1)}, u32[]{:S(2)}, u32[]{:S(2)}) collective-permute-start(f32[1,1,64,256]{3,2,0,1:T(8,128)S(1)} %get-tuple-element.162), channel_id=1, source_target_pairs={{0,4},{4,8},{8,12},{12,16},{16,20},{20,24},{24,28},{28,0},{1,5},{5... | collective-permute-start | bytes 196616 | tf_op jit(solution)/shard_map/ppermute | solution.py:25
  214.8 7.4 %collective-permute-start.25 = (f32[1,1,64,256]{3,2,0,1:T(8,128)S(1)}, f32[1,1,64,256]{3,2,0,1:T(8,128)S(1)}, u32[]{:S(2)}, u32[]{:S(2)}) collective-permute-start(f32[1,1,64,256]{3,2,0,1:T(8,128)S(1)} %get-tuple-element.163), channel_id=1, source_target_pairs={{4,0},{8,4},{12,8},{16,12},{20,16},{24,20},{28,24},{0,28},{5,1},{9... | collective-permute-start | bytes 196616 | tf_op jit(solution)/shard_map/ppermute | solution.py:27
  270.8 7.1 %collective-permute-start.28 = (f32[1,1,64,256]{3,2,0,1:T(8,128)S(1)}, f32[1,1,64,256]{3,2,0,1:T(8,128)S(1)}, u32[]{:S(2)}, u32[]{:S(2)}) collective-permute-start(f32[1,1,64,256]{3,2,0,1:T(8,128)S(1)} %get-tuple-element.160), channel_id=1, source_target_pairs={{0,4},{4,8},{8,12},{12,16},{16,20},{20,24},{24,28},{28,0},{1,5},{5... | collective-permute-start | bytes 196616 | tf_op jit(solution)/shard_map/ppermute | solution.py:25
  273.1 5.0 %collective-permute-start.29 = (f32[1,1,64,256]{3,2,0,1:T(8,128)S(1)}, f32[1,1,64,256]{3,2,0,1:T(8,128)S(1)}, u32[]{:S(2)}, u32[]{:S(2)}) collective-permute-start(f32[1,1,64,256]{3,2,0,1:T(8,128)S(1)} %get-tuple-element.161), channel_id=1, source_target_pairs={{4,0},{8,4},{12,8},{16,12},{20,16},{24,20},{28,24},{0,28},{5,1},{9... | collective-permute-start | bytes 196616 | tf_op jit(solution)/shard_map/ppermute | solution.py:27
  (19 other events, 174.3 us)
where the time goes:
time: 335 us; the launch traced here: 334 us
  waiting for transfers between devices  93.3 us (28%)
  blocking collectives  81 us (24%)
  starting transfers between devices  53.8 us (16%)
  matrix products  52.6 us (16%)
  other arithmetic  36.8 us (11%)
  local copies, waits for them, and re-layouts  8.73 us (3%)
  between operations  7.75 us (2%)
    psum x2, blocking collectives, paired(): lax.psum((jnp.sum(residual_now * scaled_vec), jnp.sum(scaled_vec * mapped...  81 us
    ppermute x16, waiting for transfers between devices, extended_2(): lax.ppermute(tail, axis, [(i, (i + 1) % count) for i in range(count)])  78.2 us
    dot_general x14, matrix products, deposit_plane(): lax.dot_general(split_weight, weight_x, (((1,), (1,)), ((), ())), preferr...  52.6 us
    ppermute x16, starting transfers between devices, extended_2(): lax.ppermute(head, axis, [((i + 1) % count, i) for i in range(count)])  45.5 us
    ppermute x16, waiting for transfers between devices, extended_2(): lax.ppermute(head, axis, [((i + 1) % count, i) for i in range(count)])  15.1 us
    div x15, other arithmetic, plane_weights(): return jnp.where(active, tap_weight(distance), 0.0) / norm_value[None, :]  10.9 us
    ppermute x16, starting transfers between devices, extended_2(): lax.ppermute(tail, axis, [(i, (i + 1) % count) for i in range(count)])  8.29 us
  transfers between devices with their start and end apart: 32, of which 20 were waited for; matrix products, arithmetic and copies ran while one was open for 2% of the time, Pallas kernels for 0%

commit v1 on v0

v1 whole, which is shorter than its diff:
```python
import functools

import jax
import jax.numpy as jnp
from jax import lax
from jax.experimental import pallas as pl
from jax.experimental.pallas import tpu as pltpu
from jax.sharding import PartitionSpec as P

SWEEPS = 3
REACH = 3
HALO = SWEEPS + 1
EDGE = 2 * HALO
CHUNK = 1024
smooth_rate = 0.15
stiffness = 0.002
F32 = jnp.float32
MESH = pl.DeviceIdType.MESH


def tap(distance):
    return jnp.exp(-0.5 * distance * distance)


def split_cell(cell, ny, nx):
    if ny & (ny - 1) == 0 and nx & (nx - 1) == 0:
        sx, sy = nx.bit_length() - 1, ny.bit_length() - 1
        return (
            lax.shift_right_logical(cell, sx + sy),
            lax.shift_right_logical(cell, sx) & (ny - 1),
            cell & (nx - 1),
        )
    row = lax.div(cell, nx)
    return lax.div(row, ny), lax.rem(row, ny), lax.rem(cell, nx)


def step_kernel(
    ngz, ngy, nz, ny, nx, slots,
    pk_ref, div_ref, p_ref, den_ref,
    gf_ref, mom_ref, out_ref, res_ref,
    near, wz_ref, wy_ref, wx_ref, dep, fld, tile_in,
    halo_z, halo_y, mob, face_z, face_s, face_n, face_w, face_e, diag,
    r_ref, z_ref, q_ref, w_ref, aw_ref, tile_y, tile_z, red_y, red_z,
    near_send, near_recv, tile_send, tile_recv, hz_send, hz_recv, hy_send, hy_recv,
    ry_send, ry_recv, rz_send, rz_recv,
):
    gz, gy = lax.axis_index("gz"), lax.axis_index("gy")
    planes, rows = nz + 2 * HALO, ny + EDGE
    total_y = ngy * ny
    first = gy * ny
    up, down = lax.rem(gz + 1, ngz), lax.rem(gz + ngz - 1, ngz)
    has_s, has_n = gy > 0, gy < ngy - 1

    barrier = pltpu.get_barrier_semaphore()
    for d in range(1, ngz):
        pl.semaphore_signal(barrier, inc=1, device_id={"gz": lax.rem(gz + d, ngz)}, device_id_type=MESH)
    for d in range(1, ngy):
        pl.semaphore_signal(barrier, inc=1, device_id={"gy": lax.rem(gy + d, ngy)}, device_id_type=MESH)
    pl.semaphore_wait(barrier, ngz - 1 + ngy - 1)

    def remote(src, dst, send, recv, where):
        return pltpu.make_async_remote_copy(
            src_ref=src, dst_ref=dst, send_sem=send, recv_sem=recv, device_id=where, device_id_type=MESH
        )

    near_copies = [
        remote(pk_ref, near.at[0], near_send.at[0], near_recv.at[0], {"gz": up}),
        remote(pk_ref, near.at[1], near_send.at[1], near_recv.at[1], {"gz": down}),
    ]
    for c in near_copies:
        c.start()

    def halo_pair(slot, src):
        zc = [
            remote(src.at[nz - 1], halo_z.at[slot, 0], hz_send.at[slot, 0], hz_recv.at[slot, 0], {"gz": up}),
            remote(src.at[0], halo_z.at[slot, 1], hz_send.at[slot, 1], hz_recv.at[slot, 1], {"gz": down}),
        ]
        north = remote(
            src.at[:, pl.ds(ny - 8, 8), :], halo_y.at[slot, 0], hy_send.at[slot, 0], hy_recv.at[slot, 0],
            {"gy": lax.rem(gy + 1, ngy)},
        )
        south = remote(
            src.at[:, pl.ds(0, 8), :], halo_y.at[slot, 1], hy_send.at[slot, 1], hy_recv.at[slot, 1],
            {"gy": lax.rem(gy + ngy - 1, ngy)},
        )
        return zc, north, south

    def halo_start(pair):
        zc, north, south = pair
        for c in zc:
            c.start()

        @pl.when(has_n)
        def _():
            north.start()

        @pl.when(has_s)
        def _():
            south.start()

    def halo_wait(pair):
        zc, north, south = pair
        for c in zc:
            c.wait()

        @pl.when(has_n)
        def _():
            north.wait_send()
            south.wait_recv()

        @pl.when(has_s)
        def _():
            south.wait_send()
            north.wait_recv()

    pair_p, pair_d = halo_pair(0, p_ref), halo_pair(1, den_ref)
    halo_start(pair_d)
    halo_start(pair_p)

    def prepare(pk, brick):
        for at in range(0, slots, CHUNK):
            sl = pl.ds(at, CHUNK)
            cz, cy, cx = split_cell(pk[4:5, sl].astype(jnp.int32), ny, nx)
            hz, hy, hx = 0.5 - pk[5:6, sl], 0.5 - pk[6:7, sl], 0.5 - pk[7:8, sl]
            sum_z = jnp.zeros_like(hz)
            sum_y = jnp.zeros_like(hz)
            sum_x = jnp.zeros_like(hz)
            for t in range(-REACH, REACH + 1):
                sum_z = sum_z + tap(t + hz)
                iy = first + cy + t
                sum_y = sum_y + jnp.where((iy >= 0) & (iy < total_y), tap(t + hy), 0.0)
                ix = cx + t
                sum_x = sum_x + jnp.where((ix >= 0) & (ix < nx), tap(t + hx), 0.0)
            iz = lax.broadcasted_iota(jnp.int32, (planes, CHUNK), 0) - HALO - brick * nz - cz
            wz_ref[:, sl] = jnp.where(jnp.abs(iz) <= REACH, tap(iz.astype(F32) + hz), 0.0) * (1.0 / sum_z)
            row = lax.broadcasted_iota(jnp.int32, (rows, CHUNK), 0) - HALO
            iy = row - cy
            ok = (jnp.abs(iy) <= REACH) & (row + first >= 0) & (row + first < total_y)
            wy_ref[:, sl] = jnp.where(ok, tap(iy.astype(F32) + hy), 0.0) * (1.0 / sum_y)
            ix = (lax.broadcasted_iota(jnp.int32, (nx, CHUNK), 0) - cx).astype(F32)
            wx = jnp.where(jnp.abs(ix) <= REACH, tap(ix + hx), 0.0) * (1.0 / sum_x)
            wx_ref[:, sl] = wx.astype(jnp.bfloat16)

    def deposit(pk, lo, hi, add):
        def body(i, carry):
            acc = None
            for at in range(0, slots, CHUNK):
                sl = pl.ds(at, CHUNK)
                scaled = pk[0:4, sl] * wz_ref[pl.ds(i, 1), sl]
                wy = wy_ref[:, sl]
                lhs = jnp.concatenate([scaled[k : k + 1] * wy for k in range(4)], axis=0).astype(jnp.bfloat16)
                part = lax.dot_general(
                    lhs, wx_ref[:, sl], (((1,), (1,)), ((), ())), preferred_element_type=F32
                )
                acc = part if acc is None else acc + part
            acc = acc.reshape(4, rows, nx)
            dep[i] = dep[i] + acc if add else acc
            return carry

        lax.fori_loop(lo, hi, body, 0)

    dep[0] = jnp.zeros((4, rows, nx), F32)
    dep[planes - 1] = jnp.zeros((4, rows, nx), F32)
    prepare(pk_ref, 0)
    deposit(pk_ref, HALO - REACH, planes - (HALO - REACH), False)
    for c in near_copies:
        c.wait()

    def tile_copies(half):
        part = pl.ds(half * (planes // 2), planes // 2)
        north = remote(
            dep.at[part, :, pl.ds(ny, EDGE), :], tile_in.at[0, part], tile_send.at[half, 0],
            tile_recv.at[half, 0], {"gy": lax.rem(gy + 1, ngy)},
        )
        south = remote(
            dep.at[part, :, pl.ds(0, EDGE), :], tile_in.at[1, part], tile_send.at[half, 1],
            tile_recv.at[half, 1], {"gy": lax.rem(gy + ngy - 1, ngy)},
        )
        return [], north, south

    prepare(near.at[0], -1)
    deposit(near.at[0], 0, HALO + REACH, True)
    tiles0, tiles1 = tile_copies(0), tile_copies(1)
    halo_start(tiles0)
    prepare(near.at[1], 1)
    deposit(near.at[1], planes - HALO - REACH, planes, True)
    halo_start(tiles1)
    halo_wait(tiles0)
    halo_wait(tiles1)

    @pl.when(has_s)
    def _():
        dep[:, :, 0:EDGE, :] = dep[:, :, 0:EDGE, :] + tile_in[0]

    @pl.when(has_n)
    def _():
        dep[:, :, ny : ny + EDGE, :] = dep[:, :, ny : ny + EDGE, :] + tile_in[1]

    def shifts_x(v):
        lane = lax.broadcasted_iota(jnp.int32, v.shape, 1)
        west = jnp.where(lane > 0, pltpu.roll(v, 1, 1), 0.0)
        east = jnp.where(lane < nx - 1, pltpu.roll(v, nx - 1, 1), 0.0)
        return west, east

    def sweep(src, dst, lo, hi):
        place = lax.broadcasted_iota(jnp.int32, (rows, nx), 0) - HALO + first
        lane = lax.broadcasted_iota(jnp.int32, (rows, nx), 1)
        count = (
            2.0
            + (place >= 1).astype(F32)
            + (place < total_y - 1).astype(F32)
            + (lane >= 1).astype(F32)
            + (lane < nx - 1).astype(F32)
        )
        inside = (place >= 0) & (place < total_y)
        scale_c = jnp.where(inside, 1.0 - smooth_rate * count, 0.0)
        scale_n = jnp.where(inside, smooth_rate, 0.0)

        def body(i, carry):
            for k in range(4):
                c = src[i, k]
                west, east = shifts_x(c)
                beside = (
                    src[i - 1, k] + src[i + 1, k] + pltpu.roll(c, 1, 0) + pltpu.roll(c, rows - 1, 0) + west + east
                )
                dst[i, k] = scale_c * c + scale_n * beside
            return carry

        lax.fori_loop(lo, hi, body, 0)

    bufs = [dep, fld]
    for s in range(SWEEPS):
        sweep(bufs[s % 2], bufs[(s + 1) % 2], s + 1, planes - s - 1)
    f = bufs[SWEEPS % 2]

    def own(v, shift=0):
        return pltpu.roll(v, rows - HALO - shift, 0)[0:ny]

    halo_wait(pair_d)
    halo_wait(pair_p)
    for z in range(-1, nz + 1):
        g = own(1.0 / (1.0 + f[z + HALO, 0]))
        if 0 <= z < nz:
            gf_ref[z] = g
            for k in range(3):
                mom_ref[z, k] = own(f[z + HALO, k + 1])
            den = den_ref[z]
        else:
            den = halo_z[1, 0 if z < 0 else 1]
        mob[z + 1] = g / den

    row_id = lax.broadcasted_iota(jnp.int32, (ny, nx), 0)

    def shifts_y(v, south_row, north_row):
        south = jnp.where(row_id == 0, south_row, pltpu.roll(v, 1, 0))
        north = jnp.where(row_id == ny - 1, north_row, pltpu.roll(v, ny - 1, 0))
        return south, north

    def halo_rows(slot, z):
        s = jnp.where(has_s, halo_y[slot, 0, z, 7:8, :], 0.0)
        n = jnp.where(has_n, halo_y[slot, 1, z, 0:1, :], 0.0)
        return s, n

    def apply(v, slot, z):
        c = v[z]
        below = v[z - 1] if z > 0 else halo_z[slot, 0]
        above = v[z + 1] if z < nz - 1 else halo_z[slot, 1]
        south, north = shifts_y(c, *halo_rows(slot, z))
        west, east = shifts_x(c)
        coupled = (
            face_z[z] * below + face_z[z + 1] * above + face_s[z] * south + face_n[z] * north
            + face_w[z] * west + face_e[z] * east
        )
        return diag[z] * c - coupled

    for z in range(nz + 1):
        face_z[z] = 0.5 * (mob[z] + mob[z + 1])
    for z in range(nz):
        m = mob[z + 1]
        gs = f[z + HALO, 0, HALO - 1 : HALO, :]
        gn = f[z + HALO, 0, HALO + ny : HALO + ny + 1, :]
        ms = jnp.where(has_s, 1.0 / (1.0 + gs) / halo_y[1, 0, z, 7:8, :], 0.0)
        mn = jnp.where(has_n, 1.0 / (1.0 + gn) / halo_y[1, 1, z, 0:1, :], 0.0)
        south, north = shifts_y(m, ms, mn)
        west, east = shifts_x(m)
        fs, fn, fw, fe = 0.5 * (m + south), 0.5 * (m + north), 0.5 * (m + west), 0.5 * (m + east)
        face_s[z], face_n[z], face_w[z], face_e[z] = fs, fn, fw, fe
        dg = stiffness * m + face_z[z] + face_z[z + 1] + fs + fn + fw + fe
        diag[z] = dg
        mz_d, mz_u = own(f[z + HALO - 1, 1]), own(f[z + HALO + 1, 1])
        my = f[z + HALO, 2]
        xw, xe = shifts_x(own(f[z + HALO, 3]))
        spread = 0.5 * (mz_u - mz_d) + 0.5 * (own(my, 1) - own(my, -1)) + 0.5 * (xe - xw)
        r0 = div_ref[z] - spread - apply(p_ref, 0, z)
        r_ref[z] = r0
        z_ref[z] = r0 / dg

    pair_z = halo_pair(2, z_ref)
    halo_start(pair_z)
    halo_wait(pair_z)

    def fold(v):
        part = jnp.sum(v, axis=0, keepdims=True)
        out = part[:, 0:128]
        for at in range(128, nx, 128):
            out = out + part[:, at : at + 128]
        return out

    def reduce_y(n, a, b):
        ids = lax.broadcasted_iota(jnp.int32, (8, 128), 0)
        tile_y[n] = jnp.where(ids == 0, a, jnp.where(ids == 1, b, 0.0))
        copies = [
            remote(
                tile_y.at[n], red_y.at[n, d - 1], ry_send.at[n, d - 1], ry_recv.at[n, d - 1],
                {"gy": lax.rem(gy + d, ngy)},
            )
            for d in range(1, ngy)
        ]
        for c in copies:
            c.start()
        return copies

    def reduce_z(n, copies):
        for c in copies:
            c.wait()
        total = tile_y[n]
        for d in range(1, ngy):
            total = total + red_y[n, d - 1]
        tile_z[n] = total
        copies = [
            remote(
                tile_z.at[n], red_z.at[n, d - 1], rz_send.at[n, d - 1], rz_recv.at[n, d - 1],
                {"gz": lax.rem(gz + d, ngz)},
            )
            for d in range(1, ngz)
        ]
        for c in copies:
            c.start()
        return copies

    def reduce_end(n, copies):
        for c in copies:
            c.wait()
        total = tile_z[n]
        for d in range(1, ngz):
            total = total + red_z[n, d - 1]
        total = jnp.sum(total, axis=1, keepdims=True)
        return total[0:1], total[1:2]

    acc_a = acc_b = jnp.zeros((ny, nx), F32)
    for z in range(nz):
        q = apply(z_ref, 2, z)
        q_ref[z] = q
        w_ref[z] = q / diag[z]
        acc_a = acc_a + r_ref[z] * z_ref[z]
        acc_b = acc_b + z_ref[z] * q
    copies = reduce_y(0, fold(acc_a), fold(acc_b))
    pair_w = halo_pair(3, w_ref)
    halo_start(pair_w)
    copies = reduce_z(0, copies)
    halo_wait(pair_w)
    for z in range(nz):
        aw_ref[z] = apply(w_ref, 3, z)
    norm0, curve0 = reduce_end(0, copies)
    step0 = norm0 / curve0
    acc_a = acc_b = jnp.zeros((ny, nx), F32)
    for z in range(nz):
        r1 = r_ref[z] - step0 * q_ref[z]
        res_ref[z] = r1
        z1 = r1 / diag[z]
        az1 = q_ref[z] - step0 * aw_ref[z]
        acc_a = acc_a + r1 * z1
        acc_b = acc_b + z1 * az1
        w_ref[z] = z1
        aw_ref[z] = az1
    copies = reduce_z(1, reduce_y(1, fold(acc_a), fold(acc_b)))
    norm1, curve1 = reduce_end(1, copies)
    beta = norm1 / norm0
    step1 = norm1 / (curve1 - beta * norm1 / step0)
    for z in range(nz):
        d0 = z_ref[z]
        out_ref[z] = p_ref[z] + step0 * d0 + step1 * (w_ref[z] + beta * d0)
        res_ref[z] = res_ref[z] - step1 * (aw_ref[z] + beta * q_ref[z])


def on_device(ngz, ngy, parcel_cell, parcel_offset, parcel_volume, parcel_force, brick_counts,
              divergence, pressure_prev, gas_density):
    nz, ny, nx = divergence.shape
    slots = parcel_cell.shape[0]
    live = jnp.arange(slots, dtype=jnp.int32) < brick_counts[0, 0]
    volume = jnp.where(live, parcel_volume, 0.0)[None, :]
    packed = jnp.concatenate(
        [volume, volume * parcel_force, parcel_cell.astype(F32)[None, :], parcel_offset], axis=0
    )
    planes, rows = nz + 2 * HALO, ny + EDGE
    field = jax.ShapeDtypeStruct((nz, ny, nx), F32)
    own = pltpu.VMEM((nz, ny, nx), F32)
    dma = pltpu.SemaphoreType.DMA
    vmem = pl.BlockSpec(memory_space=pltpu.VMEM)
    return pl.pallas_call(
        functools.partial(step_kernel, ngz, ngy, nz, ny, nx, slots),
        out_shape=(field, jax.ShapeDtypeStruct((nz, 3, ny, nx), F32), field, field),
        in_specs=[vmem] * 4,
        out_specs=(vmem,) * 4,
        scratch_shapes=[
            pltpu.VMEM((2, 8, slots), F32),
            pltpu.VMEM((planes, slots), F32),
            pltpu.VMEM((rows, slots), F32),
            pltpu.VMEM((nx, slots), jnp.bfloat16),
            pltpu.VMEM((planes, 4, rows, nx), F32),
            pltpu.VMEM((planes, 4, rows, nx), F32),
            pltpu.VMEM((2, planes, 4, EDGE, nx), F32),
            pltpu.VMEM((4, 2, ny, nx), F32),
            pltpu.VMEM((4, 2, nz, 8, nx), F32),
            pltpu.VMEM((nz + 2, ny, nx), F32),
            pltpu.VMEM((nz + 1, ny, nx), F32),
            own, own, own, own, own,
            own, own, own, own, own,
            pltpu.VMEM((2, 8, 128), F32),
            pltpu.VMEM((2, 8, 128), F32),
            pltpu.VMEM((2, ngy - 1, 8, 128), F32),
            pltpu.VMEM((2, ngz - 1, 8, 128), F32),
            dma((2,)), dma((2,)),
            dma((2, 2)), dma((2, 2)),
            dma((4, 2)), dma((4, 2)), dma((4, 2)), dma((4, 2)),
            dma((2, ngy - 1)), dma((2, ngy - 1)), dma((2, ngz - 1)), dma((2, ngz - 1)),
        ],
        compiler_params=pltpu.CompilerParams(
            collective_id=0, has_side_effects=True, vmem_limit_bytes=60 * 1024 * 1024
        ),
    )(packed, divergence, pressure_prev, gas_density)


def solution(mesh):
    ngz, ngy = mesh.shape["gz"], mesh.shape["gy"]
    return jax.shard_map(
        functools.partial(on_device, ngz, ngy),
        mesh=mesh,
        in_specs=(
            P(("gz", "gy")),
            P(None, ("gz", "gy")),
            P(("gz", "gy")),
            P(None, ("gz", "gy")),
            P("gz", "gy"),
            P("gz", "gy", None),
            P("gz", "gy", None),
            P("gz", "gy", None),
        ),
        out_specs=(
            P("gz", "gy", None),
            P("gz", None, "gy", None),
            P("gz", "gy", None),
            P("gz", "gy", None),
        ),
        check_vma=False,
    )
```

time: 335 us -> 83.9 us (0.25)
  waiting for transfers between devices: 93.3 us -> 0 us
  blocking collectives: 81 us -> 0 us
  Pallas kernels: 0 us -> 72.1 us
  starting transfers between devices: 53.8 us -> 0 us
  matrix products: 52.6 us -> 0 us
  other arithmetic: 36.8 us -> 3.86 us
  between operations: 7.75 us -> 1.29 us
    ppermute x32 -> x0, waiting for transfers between devices: 93.3 us -> none  [the longest x16 78.2 us: extended_2(): lax.ppermute(tail, axis, [(i, (i + 1) % count) for i in range(count)])]
    psum x2 -> x0, blocking collectives: 81 us -> none  [paired(): lax.psum((jnp.sum(residual_now * scaled_vec), jnp.sum(scaled_vec * mapped...]
    pallas_call x0 -> x1, Pallas kernels: none -> 72.1 us  [on_device(): pl.pallas_call(functools.partial(step_kernel, ngz, ngy, nz, ny, nx, slots...]
    ppermute x32 -> x0, starting transfers between devices: 53.8 us -> none  [the longest x16 45.5 us: extended_2(): lax.ppermute(head, axis, [((i + 1) % count, i) for i in range(count)])]
    dot_general x14 -> x0, matrix products: 52.6 us -> none  [deposit_plane(): lax.dot_general(split_weight, weight_x, (((1,), (1,)), ((), ())), preferr...]
    div x18 -> x0, other arithmetic: 15.1 us -> none  [the longest x15 10.9 us: plane_weights(): return jnp.where(active, tap_weight(distance), 0.0) / norm_value[None, :]]
    add x12 -> x0, other arithmetic: 7.15 us -> none  [the longest x3 3.47 us: smooth_once(): return centre + smooth_rate * (beside - neighbour_count * centre)]
    reduce_sum x2 -> x0, other arithmetic: 4.73 us -> none  [paired(): jnp.sum(scaled_vec * mapped_vec)]
  transfers between devices with their start and end apart: 32 -> 0, of which waited for: 20 -> 0; matrix products, arithmetic and copies ran while one was open for 2% -> 0% of each run, Pallas kernels for 0% -> 0%
where the time goes in v1:
time: 83.9 us; the launch traced here: 83.5 us
  Pallas kernels  72.1 us (86%)
  local copies, waits for them, and re-layouts  6.25 us (7%)
  other arithmetic  3.86 us (5%)
  between operations  1.29 us (2%)
    pallas_call x1, Pallas kernels, on_device(): pl.pallas_call(functools.partial(step_kernel, ngz, ngy, nz, ny, nx, slots...  72.1 us
    unnamed x8, local copies, waits for them, and re-layouts  6.25 us

profile of v1, /device:TPU:0, one launch (start us, length us, event | category | flops | bytes accessed | tf_op | source)
XLA Modules:
  0.0 83.5 jit_solution(16459453676487767074)
XLA Ops:
  1.3 0.7 fusion
  2.0 0.7 convert_element_type.3
  2.7 0.9 %broadcast_multiply_fusion = f32[3,4096]{1,0:T(4,128)S(1)} fusion(f32[3,4096]{1,0:T(4,128)} %param.11, f32[4096]{0:T(1024)S(1)} %fusion), kind=kLoop, calls=%fused_computation.1 | loop fusion | flops 12288 | bytes 114688 | tf_op jit(solution)/shard_map/mul | solution.py:393
  3.6 1.6 %pad_maximum_fusion.pk_ref = f32[8,4096]{1,0:T(8,128)} fusion(f32[3,4096]{1,0:T(4,128)} %param.9, f32[1,4096]{1,0:T(1,128)S(1)} %bitcast.5, f32[3,4096]{1,0:T(4,128)S(1)} %broadcast_multiply_fusion, f32[1,4096]{1,0:T(1,128)S(1)} %bitcast.4), kind=kLoop, calls=%fused_computation | loop fusion | flops 98304 | bytes 262144 | tf_op jit(solution)/shard_map/concatenate | solution.py:392
  5.1 72.1 %shard_map.111 = (f32[8,64,256]{2,1,0:T(8,128)}, f32[8,3,64,256]{3,2,1,0:T(8,128)}, f32[8,64,256]{2,1,0:T(8,128)}, f32[8,64,256]{2,1,0:T(8,128)}) custom-call(f32[8,4096]{1,0:T(8,128)} %pad_maximum_fusion.pk_ref, f32[8,64,256]{2,1,0:T(8,128)} %div_ref.1, f32[8,64,256]{2,1,0:T(8,128)} %p_ref.1, f32[8,64,256]{2,1,0:T(8,128)} %den_ref.1), custom_call_target="tpu_custom_call" | custom-call | tf_op jit(solution)/shard_map/pallas_call | solution.py:400
  77.2 1.9 %copy.17 = f32[8,64,256]{2,1,0:T(8,128)} copy(f32[8,64,256]{2,1,0:T(8,128)} %get-tuple-element.8) | data formatting | bytes 1048576
  79.1 0.0 copy-start.1
  79.1 0.0 copy-start
  79.1 2.8 %copy.18 = f32[8,3,64,256]{3,2,1,0:T(8,128)} copy(f32[8,3,64,256]{3,2,1,0:T(8,128)} %get-tuple-element.9) | data formatting | bytes 3145728
  81.9 0.0 copy-done.1
  81.9 0.8 copy.19
  82.7 0.0 copy-done
  82.7 0.8 copy.20
Async XLA Ops:
  79.1 2.8 %copy-start.1 = (f32[8,64,256]{2,1,0:T(8,128)S(1)}, f32[8,64,256]{2,1,0:T(8,128)}, u32[]{:S(2)}) copy-start(f32[8,64,256]{2,1,0:T(8,128)} %get-tuple-element.10) | copy-start | bytes 1572868
  79.1 3.6 %copy-start = (f32[8,64,256]{2,1,0:T(8,128)S(1)}, f32[8,64,256]{2,1,0:T(8,128)}, u32[]{:S(2)}) copy-start(f32[8,64,256]{2,1,0:T(8,128)} %get-tuple-element.11) | copy-start | bytes 1572868

commit v2 on v1

--- a/solution.py
+++ b/solution.py
@@ -1,4 +1,5 @@
 import functools
+import math
 
 import jax
 import jax.numpy as jnp
@@ -12,6 +13,8 @@
 HALO = SWEEPS + 1
 EDGE = 2 * HALO
 CHUNK = 1024
+LANES = 128
+PIECES = 4
 smooth_rate = 0.15
 stiffness = 0.002
 F32 = jnp.float32
@@ -19,7 +22,7 @@
 
 
 def tap(distance):
-    return jnp.exp(-0.5 * distance * distance)
+    return jnp.exp2((-0.5 * math.log2(math.e)) * (distance * distance))
 
 
 def split_cell(cell, ny, nx):
@@ -36,13 +39,13 @@
 
 def step_kernel(
     ngz, ngy, nz, ny, nx, slots,
-    pk_ref, div_ref, p_ref, den_ref,
-    gf_ref, mom_ref, out_ref, res_ref,
-    near, wz_ref, wy_ref, wx_ref, dep, fld, tile_in,
+    count_ref, cell_ref, off_ref, vol_ref, force_ref, div_ref, p_ref, den_ref,
+    gf_out, mom_out, p_out, res_out,
+    gf_ref, mom_ref, out_ref, res_ref, pk_ref, near, wz_ref, wy_ref, wx_ref, dep, fld, tile_in,
     halo_z, halo_y, mob, face_z, face_s, face_n, face_w, face_e, diag,
     r_ref, z_ref, q_ref, w_ref, aw_ref, tile_y, tile_z, red_y, red_z,
     near_send, near_recv, tile_send, tile_recv, hz_send, hz_recv, hy_send, hy_recv,
-    ry_send, ry_recv, rz_send, rz_recv,
+    ry_send, ry_recv, rz_send, rz_recv, out_sem,
 ):
     gz, gy = lax.axis_index("gz"), lax.axis_index("gy")
     planes, rows = nz + 2 * HALO, ny + EDGE
@@ -56,6 +59,12 @@
         pl.semaphore_signal(barrier, inc=1, device_id={"gz": lax.rem(gz + d, ngz)}, device_id_type=MESH)
     for d in range(1, ngy):
         pl.semaphore_signal(barrier, inc=1, device_id={"gy": lax.rem(gy + d, ngy)}, device_id_type=MESH)
+    live = lax.broadcasted_iota(jnp.int32, (1, slots), 1) < count_ref[0, 0]
+    volume = jnp.where(live, vol_ref[...], 0.0)
+    pk_ref[0:1] = volume
+    pk_ref[1:4] = volume * force_ref[...]
+    pk_ref[4:5] = cell_ref[...].astype(F32)
+    pk_ref[5:8] = off_ref[...]
     pl.semaphore_wait(barrier, ngz - 1 + ngy - 1)
 
     def remote(src, dst, send, recv, where):
@@ -85,9 +94,9 @@
         )
         return zc, north, south
 
-    def halo_start(pair):
+    def halo_start(pair, along_z=True):
         zc, north, south = pair
-        for c in zc:
+        for c in zc if along_z else []:
             c.start()
 
         @pl.when(has_n)
@@ -117,42 +126,44 @@
     halo_start(pair_d)
     halo_start(pair_p)
 
-    def prepare(pk, brick):
-        for at in range(0, slots, CHUNK):
-            sl = pl.ds(at, CHUNK)
-            cz, cy, cx = split_cell(pk[4:5, sl].astype(jnp.int32), ny, nx)
+    row_iota = lax.broadcasted_iota(jnp.int32, (rows, LANES), 0) - HALO
+    row_id = jnp.where((row_iota + first >= 0) & (row_iota + first < total_y), row_iota, 4 * total_y).astype(F32)
+    col_id = lax.broadcasted_iota(jnp.int32, (nx, LANES), 0).astype(F32)
+    plane_id = (lax.broadcasted_iota(jnp.int32, (planes, LANES), 0) - HALO).astype(F32)
+
+    def prepare(pk, brick, slot, at, width):
+        for off in range(0, width, LANES):
+            sl = pl.ds(pl.multiple_of(at + off, LANES), LANES)
+            cz, cy, cx = [c.astype(F32) for c in split_cell(pk[4:5, sl].astype(jnp.int32), ny, nx)]
             hz, hy, hx = 0.5 - pk[5:6, sl], 0.5 - pk[6:7, sl], 0.5 - pk[7:8, sl]
             sum_z = jnp.zeros_like(hz)
-            sum_y = jnp.zeros_like(hz)
-            sum_x = jnp.zeros_like(hz)
             for t in range(-REACH, REACH + 1):
                 sum_z = sum_z + tap(t + hz)
-                iy = first + cy + t
-                sum_y = sum_y + jnp.where((iy >= 0) & (iy < total_y), tap(t + hy), 0.0)
-                ix = cx + t
-                sum_x = sum_x + jnp.where((ix >= 0) & (ix < nx), tap(t + hx), 0.0)
-            iz = lax.broadcasted_iota(jnp.int32, (planes, CHUNK), 0) - HALO - brick * nz - cz
-            wz_ref[:, sl] = jnp.where(jnp.abs(iz) <= REACH, tap(iz.astype(F32) + hz), 0.0) * (1.0 / sum_z)
-            row = lax.broadcasted_iota(jnp.int32, (rows, CHUNK), 0) - HALO
-            iy = row - cy
-            ok = (jnp.abs(iy) <= REACH) & (row + first >= 0) & (row + first < total_y)
-            wy_ref[:, sl] = jnp.where(ok, tap(iy.astype(F32) + hy), 0.0) * (1.0 / sum_y)
-            ix = (lax.broadcasted_iota(jnp.int32, (nx, CHUNK), 0) - cx).astype(F32)
-            wx = jnp.where(jnp.abs(ix) <= REACH, tap(ix + hx), 0.0) * (1.0 / sum_x)
-            wx_ref[:, sl] = wx.astype(jnp.bfloat16)
-
-    def deposit(pk, lo, hi, add):
+
+            def masked(ids, home, half):
+                t = ids - home
+                return jnp.where(jnp.abs(t) <= REACH, tap(t + half), 0.0)
+
+            wz_ref[slot, :, sl] = masked(plane_id - brick * nz, cz, hz) * (1.0 / sum_z)
+            wy = masked(row_id, cy, hy)
+            wy_ref[slot, :, sl] = wy * (1.0 / jnp.sum(wy, axis=0, keepdims=True))
+            wx = masked(col_id, cx, hx)
+            wx_ref[slot, :, sl] = (wx * (1.0 / jnp.sum(wx, axis=0, keepdims=True))).astype(jnp.bfloat16)
+
+    def deposit(pk, slot, lo, hi, add, beside=None):
         def body(i, carry):
             acc = None
             for at in range(0, slots, CHUNK):
                 sl = pl.ds(at, CHUNK)
-                scaled = pk[0:4, sl] * wz_ref[pl.ds(i, 1), sl]
-                wy = wy_ref[:, sl]
+                scaled = pk[0:4, sl] * wz_ref[slot, pl.ds(i, 1), sl]
+                wy = wy_ref[slot, :, sl]
                 lhs = jnp.concatenate([scaled[k : k + 1] * wy for k in range(4)], axis=0).astype(jnp.bfloat16)
                 part = lax.dot_general(
-                    lhs, wx_ref[:, sl], (((1,), (1,)), ((), ())), preferred_element_type=F32
+                    lhs, wx_ref[slot, :, sl], (((1,), (1,)), ((), ())), preferred_element_type=F32
                 )
                 acc = part if acc is None else acc + part
+            if beside is not None:
+                beside(i - lo)
             acc = acc.reshape(4, rows, nx)
             dep[i] = dep[i] + acc if add else acc
             return carry
@@ -161,10 +172,23 @@
 
     dep[0] = jnp.zeros((4, rows, nx), F32)
     dep[planes - 1] = jnp.zeros((4, rows, nx), F32)
-    prepare(pk_ref, 0)
-    deposit(pk_ref, HALO - REACH, planes - (HALO - REACH), False)
+    piece = slots // nz
+
+    def prepare_own(i, carry):
+        prepare(pk_ref, 0, 0, i * piece, piece)
+        return carry
+
+    lax.fori_loop(0, nz, prepare_own, 0)
+
+    def prepare_near(i):
+        prepare(near.at[0], -1, 1, i * piece, piece)
+        prepare(near.at[1], 1, 2, i * piece, piece)
+
+    split_at = planes - (HALO - REACH) - nz
+    deposit(pk_ref, 0, HALO - REACH, split_at, False)
     for c in near_copies:
         c.wait()
+    deposit(pk_ref, 0, split_at, planes - (HALO - REACH), False, prepare_near)
 
     def tile_copies(half):
         part = pl.ds(half * (planes // 2), planes // 2)
@@ -178,29 +202,33 @@
         )
         return [], north, south
 
-    prepare(near.at[0], -1)
-    deposit(near.at[0], 0, HALO + REACH, True)
+    deposit(near.at[0], 1, 0, HALO + REACH, True)
     tiles0, tiles1 = tile_copies(0), tile_copies(1)
     halo_start(tiles0)
-    prepare(near.at[1], 1)
-    deposit(near.at[1], planes - HALO - REACH, planes, True)
+    deposit(near.at[1], 2, planes - HALO - REACH, planes, True)
     halo_start(tiles1)
-    halo_wait(tiles0)
-    halo_wait(tiles1)
-
-    @pl.when(has_s)
-    def _():
-        dep[:, :, 0:EDGE, :] = dep[:, :, 0:EDGE, :] + tile_in[0]
-
-    @pl.when(has_n)
-    def _():
-        dep[:, :, ny : ny + EDGE, :] = dep[:, :, ny : ny + EDGE, :] + tile_in[1]
+
+    def add_tiles(half):
+        part = pl.ds(half * (planes // 2), planes // 2)
+
+        @pl.when(has_s)
+        def _():
+            dep[part, :, 0:EDGE, :] = dep[part, :, 0:EDGE, :] + tile_in[0, part]
+
+        @pl.when(has_n)
+        def _():
+            dep[part, :, ny : ny + EDGE, :] = dep[part, :, ny : ny + EDGE, :] + tile_in[1, part]
 
     def shifts_x(v):
-        lane = lax.broadcasted_iota(jnp.int32, v.shape, 1)
-        west = jnp.where(lane > 0, pltpu.roll(v, 1, 1), 0.0)
-        east = jnp.where(lane < nx - 1, pltpu.roll(v, nx - 1, 1), 0.0)
-        return west, east
+        lane = lax.broadcasted_iota(jnp.int32, (v.shape[0], LANES), 1)
+        parts = [v[:, at : at + LANES] for at in range(0, nx, LANES)]
+        ups = [pltpu.roll(part, 1, 1) for part in parts]
+        downs = [pltpu.roll(part, LANES - 1, 1) for part in parts]
+        west = [jnp.where(lane == 0, ups[n - 1] if n else 0.0, u) for n, u in enumerate(ups)]
+        east = [
+            jnp.where(lane == LANES - 1, downs[n + 1] if n + 1 < len(parts) else 0.0, u) for n, u in enumerate(downs)
+        ]
+        return jnp.concatenate(west, axis=1), jnp.concatenate(east, axis=1)
 
     def sweep(src, dst, lo, hi):
         place = lax.broadcasted_iota(jnp.int32, (rows, nx), 0) - HALO + first
@@ -229,7 +257,13 @@
         lax.fori_loop(lo, hi, body, 0)
 
     bufs = [dep, fld]
-    for s in range(SWEEPS):
+    halo_wait(tiles0)
+    add_tiles(0)
+    sweep(dep, fld, 1, planes // 2 - 1)
+    halo_wait(tiles1)
+    add_tiles(1)
+    sweep(dep, fld, planes // 2 - 1, planes - 1)
+    for s in range(1, SWEEPS):
         sweep(bufs[s % 2], bufs[(s + 1) % 2], s + 1, planes - s - 1)
     f = bufs[SWEEPS % 2]
 
@@ -249,11 +283,17 @@
             den = halo_z[1, 0 if z < 0 else 1]
         mob[z + 1] = g / den
 
-    row_id = lax.broadcasted_iota(jnp.int32, (ny, nx), 0)
+    early = [
+        pltpu.make_async_copy(gf_ref, gf_out, out_sem.at[0]),
+        pltpu.make_async_copy(mom_ref, mom_out, out_sem.at[1]),
+    ]
+    for c in early:
+        c.start()
+    own_row = lax.broadcasted_iota(jnp.int32, (ny, nx), 0)
 
     def shifts_y(v, south_row, north_row):
-        south = jnp.where(row_id == 0, south_row, pltpu.roll(v, 1, 0))
-        north = jnp.where(row_id == ny - 1, north_row, pltpu.roll(v, ny - 1, 0))
+        south = jnp.where(own_row == 0, south_row, pltpu.roll(v, 1, 0))
+        north = jnp.where(own_row == ny - 1, north_row, pltpu.roll(v, ny - 1, 0))
         return south, north
 
     def halo_rows(slot, z):
@@ -275,7 +315,9 @@
 
     for z in range(nz + 1):
         face_z[z] = 0.5 * (mob[z] + mob[z + 1])
-    for z in range(nz):
+    order = [0, nz - 1] + list(range(1, nz - 1))
+    pair_z, pair_w = halo_pair(2, z_ref), halo_pair(3, w_ref)
+    for z in order:
         m = mob[z + 1]
         gs = f[z + HALO, 0, HALO - 1 : HALO, :]
         gn = f[z + HALO, 0, HALO + ny : HALO + ny + 1, :]
@@ -294,9 +336,11 @@
         r0 = div_ref[z] - spread - apply(p_ref, 0, z)
         r_ref[z] = r0
         z_ref[z] = r0 / dg
-
-    pair_z = halo_pair(2, z_ref)
-    halo_start(pair_z)
+        if z == nz - 1:
+            for c in pair_z[0]:
+                c.start()
+
+    halo_start(pair_z, False)
     halo_wait(pair_z)
 
     def fold(v):
@@ -348,15 +392,17 @@
         return total[0:1], total[1:2]
 
     acc_a = acc_b = jnp.zeros((ny, nx), F32)
-    for z in range(nz):
+    for z in order:
         q = apply(z_ref, 2, z)
         q_ref[z] = q
         w_ref[z] = q / diag[z]
+        if z == nz - 1:
+            for c in pair_w[0]:
+                c.start()
         acc_a = acc_a + r_ref[z] * z_ref[z]
         acc_b = acc_b + z_ref[z] * q
     copies = reduce_y(0, fold(acc_a), fold(acc_b))
-    pair_w = halo_pair(3, w_ref)
-    halo_start(pair_w)
+    halo_start(pair_w, False)
     copies = reduce_z(0, copies)
     halo_wait(pair_w)
     for z in range(nz):
@@ -381,32 +427,59 @@
         d0 = z_ref[z]
         out_ref[z] = p_ref[z] + step0 * d0 + step1 * (w_ref[z] + beta * d0)
         res_ref[z] = res_ref[z] - step1 * (aw_ref[z] + beta * q_ref[z])
+    late = [
+        pltpu.make_async_copy(out_ref, p_out, out_sem.at[2]),
+        pltpu.make_async_copy(res_ref, res_out, out_sem.at[3]),
+    ]
+    for c in late:
+        c.start()
+    for c in early + late:
+        c.wait()
+
+
+def pass_kernel(*refs):
+    ins, outs, bufs, (got, put) = refs[0:4], refs[4:8], refs[8:12], refs[12:]
+    ways = []
+    for n in range(4):
+        size = ins[n].shape[0] // PIECES
+        for h in range(PIECES):
+            part = pl.ds(h * size, size)
+            ways.append((
+                pltpu.make_async_copy(ins[n].at[part], bufs[n].at[part], got.at[n, h]),
+                pltpu.make_async_copy(bufs[n].at[part], outs[n].at[part], put.at[n, h]),
+            ))
+    for first, _ in ways:
+        first.start()
+    for first, second in ways:
+        first.wait()
+        second.start()
+    for _, second in ways:
+        second.wait()
 
 
 def on_device(ngz, ngy, parcel_cell, parcel_offset, parcel_volume, parcel_force, brick_counts,
               divergence, pressure_prev, gas_density):
     nz, ny, nx = divergence.shape
     slots = parcel_cell.shape[0]
-    live = jnp.arange(slots, dtype=jnp.int32) < brick_counts[0, 0]
-    volume = jnp.where(live, parcel_volume, 0.0)[None, :]
-    packed = jnp.concatenate(
-        [volume, volume * parcel_force, parcel_cell.astype(F32)[None, :], parcel_offset], axis=0
-    )
     planes, rows = nz + 2 * HALO, ny + EDGE
     field = jax.ShapeDtypeStruct((nz, ny, nx), F32)
     own = pltpu.VMEM((nz, ny, nx), F32)
     dma = pltpu.SemaphoreType.DMA
     vmem = pl.BlockSpec(memory_space=pltpu.VMEM)
-    return pl.pallas_call(
+    hbm = pl.BlockSpec(memory_space=pl.ANY)
+    shapes = (field, jax.ShapeDtypeStruct((nz, 3, ny, nx), F32), field, field)
+    bufs = [pltpu.VMEM(shape.shape, F32) for shape in shapes]
+    made = pl.pallas_call(
         functools.partial(step_kernel, ngz, ngy, nz, ny, nx, slots),
-        out_shape=(field, jax.ShapeDtypeStruct((nz, 3, ny, nx), F32), field, field),
-        in_specs=[vmem] * 4,
-        out_specs=(vmem,) * 4,
-        scratch_shapes=[
+        out_shape=shapes,
+        in_specs=[pl.BlockSpec(memory_space=pltpu.SMEM)] + [vmem] * 7,
+        out_specs=(hbm,) * 4,
+        scratch_shapes=bufs + [
+            pltpu.VMEM((8, slots), F32),
             pltpu.VMEM((2, 8, slots), F32),
-            pltpu.VMEM((planes, slots), F32),
-            pltpu.VMEM((rows, slots), F32),
-            pltpu.VMEM((nx, slots), jnp.bfloat16),
+            pltpu.VMEM((3, planes, slots), F32),
+            pltpu.VMEM((3, rows, slots), F32),
+            pltpu.VMEM((3, nx, slots), jnp.bfloat16),
             pltpu.VMEM((planes, 4, rows, nx), F32),
             pltpu.VMEM((planes, 4, rows, nx), F32),
             pltpu.VMEM((2, planes, 4, EDGE, nx), F32),
@@ -423,12 +496,22 @@
             dma((2,)), dma((2,)),
             dma((2, 2)), dma((2, 2)),
             dma((4, 2)), dma((4, 2)), dma((4, 2)), dma((4, 2)),
-            dma((2, ngy - 1)), dma((2, ngy - 1)), dma((2, ngz - 1)), dma((2, ngz - 1)),
+            dma((2, ngy - 1)), dma((2, ngy - 1)), dma((2, ngz - 1)), dma((2, ngz - 1)), dma((4,)),
         ],
         compiler_params=pltpu.CompilerParams(
             collective_id=0, has_side_effects=True, vmem_limit_bytes=60 * 1024 * 1024
         ),
-    )(packed, divergence, pressure_prev, gas_density)
+    )(
+        brick_counts, parcel_cell[None, :], parcel_offset, parcel_volume[None, :], parcel_force,
+        divergence, pressure_prev, gas_density,
+    )
+    return pl.pallas_call(
+        pass_kernel,
+        out_shape=shapes,
+        in_specs=[hbm] * 4,
+        out_specs=(hbm,) * 4,
+        scratch_shapes=bufs + [dma((4, PIECES)), dma((4, PIECES))],
+    )(*made)
 
 
 def solution(mesh):

time: 83.9 us -> 77.4 us (0.923)
  local copies, waits for them, and re-layouts: 6.25 us -> 0 us
  other arithmetic: 3.86 us -> 0 us
  Pallas kernels: 72.1 us -> 75.9 us
    unnamed x8 -> x0, local copies, waits for them, and re-layouts: 6.25 us -> none
    pallas_call x0 -> x1, Pallas kernels: none -> 3.04 us  [on_device(): pl.pallas_call(pass_kernel, out_shape=shapes, in_specs=[hbm] * 4, out_spe...]
    concatenate x1 -> x0, other arithmetic: 1.56 us -> none  [on_device(): jnp.concatenate([volume, volume * parcel_force, parcel_cell.astype(F32)[N...]
    mul x1 -> x0, other arithmetic: 0.86 us -> none  [on_device(): volume * parcel_force]
where the time goes in v2:
time: 77.4 us; the launch traced here: 77.2 us
  Pallas kernels  75.9 us (98%)
  between operations  1.29 us (2%)
    pallas_call x1, Pallas kernels, on_device(): pl.pallas_call(functools.partial(step_kernel, ngz, ngy, nz, ny, nx, slots...  72.9 us
    pallas_call x1, Pallas kernels, on_device(): pl.pallas_call(pass_kernel, out_shape=shapes, in_specs=[hbm] * 4, out_spe...  3.04 us

profile of v2, /device:TPU:0, one launch (start us, length us, event | category | flops | bytes accessed | tf_op | source)
XLA Modules:
  0.0 77.2 jit_solution(2517966354429574008)
XLA Ops:
  1.3 72.9 %shard_map.111 = (f32[8,64,256]{2,1,0:T(8,128)}, f32[8,3,64,256]{3,2,1,0:T(8,128)}, f32[8,64,256]{2,1,0:T(8,128)}, f32[8,64,256]{2,1,0:T(8,128)}) custom-call(s32[1,1]{1,0:T(1,128)S(6)} %copy.12.count_ref, s32[1,4096]{1,0:T(1,128)} %bitcast.2, f32[3,4096]{1,0:T(4,128)} %off_ref.1, f32[1,4096]{1,0:T(1,128)} %bitcast.3, f32[3,4096]{1,0:T(4,128)} %force_ref.1, ...), custom_call_target="tpu_custom_call" | custom-call | tf_op jit(solution)/shard_map/pallas_call | solution.py:472
  74.2 3.0 %shard_map.112 = (f32[8,64,256]{2,1,0:T(8,128)}, f32[8,3,64,256]{3,2,1,0:T(8,128)}, f32[8,64,256]{2,1,0:T(8,128)}, f32[8,64,256]{2,1,0:T(8,128)}) custom-call(f32[8,64,256]{2,1,0:T(8,128)} %get-tuple-element.8.refs_0_, f32[8,3,64,256]{3,2,1,0:T(8,128)} %get-tuple-element.9.refs_1_, f32[8,64,256]{2,1,0:T(8,128)} %get-tuple-element.10.refs_2_, ...), custom_call_target="tpu_custom_call" | custom-call | tf_op jit(solution)/shard_map/pallas_call | solution.py:508

commit v3 on v2

--- a/solution.py
+++ b/solution.py
@@ -162,8 +162,8 @@
                     lhs, wx_ref[slot, :, sl], (((1,), (1,)), ((), ())), preferred_element_type=F32
                 )
                 acc = part if acc is None else acc + part
-            if beside is not None:
-                beside(i - lo)
+                if beside is not None:
+                    beside(i - lo, at // CHUNK)
             acc = acc.reshape(4, rows, nx)
             dep[i] = dep[i] + acc if add else acc
             return carry
@@ -180,9 +180,11 @@
 
     lax.fori_loop(0, nz, prepare_own, 0)
 
-    def prepare_near(i):
-        prepare(near.at[0], -1, 1, i * piece, piece)
-        prepare(near.at[1], 1, 2, i * piece, piece)
+    share = piece // (slots // CHUNK)
+
+    def prepare_near(i, n):
+        prepare(near.at[0], -1, 1, i * piece + n * share, share)
+        prepare(near.at[1], 1, 2, i * piece + n * share, share)
 
     split_at = planes - (HALO - REACH) - nz
     deposit(pk_ref, 0, HALO - REACH, split_at, False)

time: 77.4 us -> 76.9 us (level)
  no operation moved by 1% of the time
where the time goes in v3:
time: 76.9 us; the launch traced here: 76.8 us
  Pallas kernels  75.5 us (98%)
  between operations  1.29 us (2%)
    pallas_call x1, Pallas kernels, on_device(): pl.pallas_call(functools.partial(step_kernel, ngz, ngy, nz, ny, nx, slots...  72.4 us
    pallas_call x1, Pallas kernels, on_device(): pl.pallas_call(pass_kernel, out_shape=shapes, in_specs=[hbm] * 4, out_spe...  3.04 us

profile of v3, /device:TPU:0, one launch (start us, length us, event | category | flops | bytes accessed | tf_op | source)
XLA Modules:
  0.0 76.8 jit_solution(4193673635773022248)
XLA Ops:
  1.3 72.4 %shard_map.111 = (f32[8,64,256]{2,1,0:T(8,128)}, f32[8,3,64,256]{3,2,1,0:T(8,128)}, f32[8,64,256]{2,1,0:T(8,128)}, f32[8,64,256]{2,1,0:T(8,128)}) custom-call(s32[1,1]{1,0:T(1,128)S(6)} %copy.12.count_ref, s32[1,4096]{1,0:T(1,128)} %bitcast.2, f32[3,4096]{1,0:T(4,128)} %off_ref.1, f32[1,4096]{1,0:T(1,128)} %bitcast.3, f32[3,4096]{1,0:T(4,128)} %force_ref.1, ...), custom_call_target="tpu_custom_call" | custom-call | tf_op jit(solution)/shard_map/pallas_call | solution.py:474
  73.7 3.0 %shard_map.112 = (f32[8,64,256]{2,1,0:T(8,128)}, f32[8,3,64,256]{3,2,1,0:T(8,128)}, f32[8,64,256]{2,1,0:T(8,128)}, f32[8,64,256]{2,1,0:T(8,128)}) custom-call(f32[8,64,256]{2,1,0:T(8,128)} %get-tuple-element.8.refs_0_, f32[8,3,64,256]{3,2,1,0:T(8,128)} %get-tuple-element.9.refs_1_, f32[8,64,256]{2,1,0:T(8,128)} %get-tuple-element.10.refs_2_, ...), custom_call_target="tpu_custom_call" | custom-call | tf_op jit(solution)/shard_map/pallas_call | solution.py:510
